TPU v7x, 512 devices: a whole 4x8x8 slice. The times are simulated.
512 devices in a mesh: row: 32 (over y_hi, z, core), col: 16 (over y_lo, x).
Axes of the slice: x: 4, y: 8 (y_hi: 2, y_lo: 4; y = y_hi * 4 + y_lo), z: 8, core: 2. Of those that a mesh axis runs over, the one named last changes fastest.
Arguments:
- stress: float32 [256, 16384], P('col', 'row'), may hold values from -2.5 to 2.5
- state: float32 [256, 8192], P('col', 'row'), may hold values from 0 to 1
- load_rate: int32 [256, 16384], P('col', 'row'), may hold values from 0 to 2047
- a_param: float32 [8192], P('row'), may hold values from 1 to 2
- b_param: float32 [8192], P('row'), may hold values from 0.25 to 1
- near_band: bfloat16 [16384, 768], P('row'), may hold values from -0.21875 to 0.21875
- u_far: bfloat16 [64, 64, 32, 256], P('row', 'col'), may hold values from -0.1875 to 0.1875
- v_far: bfloat16 [64, 64, 32, 256], P('row', 'col'), may hold values from -0.375 to 0.375
- ranks: int32 [64, 64], P('row', 'col'), may hold values from 1 to 32, as said below
Outputs:
- new_stress: float32 [256, 16384], P('col', 'row')
- new_state: float32 [256, 8192], P('col', 'row')
Inputs may be any that keep to these rules, and one draw needn't show every extreme that they name: ranks of blocks with |I - J| <= 1 are not used; blocks with |I - J| = 2 have rank 32.
All inputs are finite; a program needn't handle non-finite values.
Results may differ from a plain program's by a relative error of at most 0.0021.
Values may be sent and summed in bfloat16 or wider, within the bound.
No kernel may reach another device: no remote copies, remote signals or barrier semaphores. Data moves between devices by JAX's collectives and lax.ppermute only.
A program may use at most 64 MiB of HBM per device.

v0:
```python
import jax
import jax.numpy as jnp
from jax import lax
from jax.sharding import PartitionSpec as P

B = 128


HSTEP = 0.2
RATE_UNIT = 1.0 / 1024.0


def broadcast(value, axis, source):
    kept = jnp.where(lax.axis_index(axis) == source, value, 0).astype(value.dtype)
    return lax.psum(kept, axis)


def extended(cells, sides, width):
    for axis, dim in sides:
        count = lax.axis_size(axis)
        ends = count - 1
        head = lax.slice_in_dim(cells, 0, width, axis=dim)
        tail = lax.slice_in_dim(cells, cells.shape[dim] - width, cells.shape[dim], axis=dim)
        cells = jnp.concatenate(
            [
                lax.ppermute(tail, axis, [(i, (i + 1) % count) for i in range(ends)]),
                cells,
                lax.ppermute(head, axis, [((i + 1) % count, i) for i in range(ends)]),
            ],
            axis=dim,
        )
    return cells


def rates_and_drift(stress_now, state_now, plate_rate, a_param, b_param):
    members = stress_now.shape[0]
    block_count = a_param.shape[0] // B
    stress_view = stress_now.reshape(members, block_count, 2, B)
    state_view = state_now.reshape(members, block_count, 1, B)
    direct_view = a_param.reshape(1, block_count, 1, B)
    evolve_view = b_param.reshape(1, block_count, B)
    slip_rate = 2.0 * jnp.exp(-state_view) * jnp.sinh(stress_view / direct_view)
    slip_speed = jnp.sqrt(jnp.sum(slip_rate * slip_rate, axis=2))
    drift = evolve_view * (jnp.exp(-state_view[:, :, 0]) - slip_speed)
    excess = (slip_rate - plate_rate.reshape(members, block_count, 2, B)).astype(jnp.bfloat16)
    return (excess.reshape(members, -1), drift.reshape(members, -1))


def far_terms(columns, u_far, v_far, ranks, row_index, col_index):
    block_rows, block_cols, rank_slots, block_dofs = u_far.shape
    members = columns.shape[0]
    grid = columns.reshape(members, block_cols, block_dofs)
    weights = jnp.einsum("mjd,ijrd->ijmr", grid, v_far, preferred_element_type=jnp.float32)
    global_rows = row_index * block_rows + jnp.arange(block_rows, dtype=jnp.int32)
    global_cols = col_index * block_cols + jnp.arange(block_cols, dtype=jnp.int32)
    distant = jnp.abs(global_rows[:, None] - global_cols[None, :]) >= 2
    active = (jnp.arange(rank_slots, dtype=jnp.int32)[None, None, :] < ranks[:, :, None]) & distant[
        :, :, None
    ]
    weights = jnp.where(active[:, :, None, :], weights, 0.0).astype(jnp.bfloat16)
    partial_value = jnp.einsum("ijmr,ijrd->mid", weights, u_far, preferred_element_type=jnp.float32)
    return partial_value.reshape(members, -1)


def near_terms(padded, first_block, near_band):
    block_dofs = near_band.shape[1] // 3
    block_rows = near_band.shape[0] // block_dofs
    members = padded.shape[0]
    segment = lax.dynamic_slice_in_dim(
        padded, first_block * block_dofs, (block_rows + 2) * block_dofs, 1
    )
    segment = segment.reshape(members, block_rows + 2, block_dofs)
    windows = jnp.concatenate(
        [segment[:, 0:block_rows], segment[:, 1 : block_rows + 1], segment[:, 2 : block_rows + 2]],
        axis=2,
    )
    band_view = near_band.reshape(block_rows, block_dofs, 3 * block_dofs)
    nearby = jnp.einsum("mik,idk->mid", windows, band_view, preferred_element_type=jnp.float32)
    return nearby.reshape(members, -1)


def local(stress, state, load_rate, a_param, b_param, near_band, u_far, v_far, ranks):
    row_index = lax.axis_index("row")
    col_index = lax.axis_index("col")
    row_ratio = lax.axis_size("row") // lax.axis_size("col")
    block_rows = u_far.shape[0]
    block_dofs = near_band.shape[1] // 3
    plate_rate = load_rate.astype(jnp.float32) * RATE_UNIT
    stress_start, state_start = (stress, state)

    def tendency(stress_now, state_now):
        excess, drift = rates_and_drift(stress_now, state_now, plate_rate, a_param, b_param)
        all_members = lax.all_gather(excess, "col", axis=0, tiled=True)
        owners = []
        for offset in range(row_ratio):
            owners.append(broadcast(all_members, "row", row_ratio * col_index + offset))
        columns = jnp.concatenate(owners, axis=1)
        partial_value = far_terms(columns, u_far, v_far, ranks, row_index, col_index)
        padded = extended(columns, (("col", 1),), block_dofs)
        on_band = col_index == row_index // row_ratio
        first_block = row_index % row_ratio * block_rows
        partial_value = partial_value + lax.cond(
            on_band,
            lambda: near_terms(padded, first_block, near_band),
            lambda: jnp.zeros_like(partial_value),
        )
        totals = lax.psum_scatter(partial_value, "col", scatter_dimension=0, tiled=True)
        return (-totals, drift)

    rate_one, drift_one = tendency(stress_start, state_start)
    stress_one = stress_start + HSTEP * rate_one
    state_one = state_start + HSTEP * drift_one
    rate_two, drift_two = tendency(stress_one, state_one)
    stress_two = 0.75 * stress_start + 0.25 * (stress_one + HSTEP * rate_two)
    state_two = 0.75 * state_start + 0.25 * (state_one + HSTEP * drift_two)
    rate_three, drift_three = tendency(stress_two, state_two)
    new_stress = stress_start / 3.0 + 2.0 / 3.0 * (stress_two + HSTEP * rate_three)
    new_state = state_start / 3.0 + 2.0 / 3.0 * (state_two + HSTEP * drift_three)
    return (new_stress, new_state)


def solution(mesh):
    return jax.shard_map(
        local,
        mesh=mesh,
        in_specs=(
            P("col", "row"),
            P("col", "row"),
            P("col", "row"),
            P("row"),
            P("row"),
            P("row", None),
            P("row", "col", None, None),
            P("row", "col", None, None),
            P("row", "col"),
        ),
        out_specs=(P("col", "row"), P("col", "row")),
        check_vma=False,
    )
```

profile of v0, /device:TPU:64, one launch (start us, length us, event | category | flops | bytes accessed | tf_op | source)
XLA Modules:
  0.0 1475.0 jit_solution(9471608002866167742)
XLA Ops:
  9.6 43.9 %all_gather.9 = bf16[256,512]{1,0:T(8,128)(2,1)S(1)} all-gather(bf16[16,512]{1,0:T(8,128)(2,1)S(1)} %fusion.59), channel_id=1, replica_groups=mesh['row'=32,'col'=16] {'col'}, dimensions={0}, use_global_device_ids=true | all-gather | bytes 278528 | tf_op jit(solution)/shard_map/all_gather | solution.py:93
  54.6 336.6 %all-reduce.11.cloned.1.call-done = (bf16[256,512]{1,0:T(8,128)(2,1)}, bf16[256,512]{1,0:T(8,128)(2,1)}) async-done(((bf16[256,512]{1,0:T(8,128)(2,1)}, bf16[256,512]{1,0:T(8,128)(2,1)}), (bf16[256,512]{1,0:T(8,128)(2,1)}, bf16[256,512]{1,0:T(8,128)(2,1)})) %all-reduce.11.cloned.1.call-update) | async-done | bytes 524304 | tf_op jit(solution)/shard_map/psum | solution.py:15
  392.1 0.9 slice.61
  393.0 1.1 pad_maximum_fusion.3
  394.1 3.4 collective-permute-start
  397.5 1.3 collective-permute-start.1
  400.5 4.1 collective-permute-done.1
  406.2 92.3 %reduce-scatter.4.cloned.1.call-done = f32[16,512]{1,0:T(8,128)} async-done(((f32[256,512]{1,0:T(8,128)}), f32[16,512]{1,0:T(8,128)}) %reduce-scatter.4.cloned.1.call-update) | async-done | bytes 32784 | tf_op jit(solution)/shard_map/reduce_scatter | solution.py:107
  499.4 38.8 %all_gather.10 = bf16[256,512]{1,0:T(8,128)(2,1)S(1)} all-gather(bf16[16,512]{1,0:T(8,128)(2,1)S(1)} %get-tuple-element.58), channel_id=1, replica_groups=mesh['row'=32,'col'=16] {'col'}, dimensions={0}, use_global_device_ids=true | all-gather | bytes 278528 | tf_op jit(solution)/shard_map/all_gather | solution.py:93
  539.1 336.2 %all-reduce.9.cloned.1.call-done = (bf16[256,512]{1,0:T(8,128)(2,1)}, bf16[256,512]{1,0:T(8,128)(2,1)}) async-done(((bf16[256,512]{1,0:T(8,128)(2,1)}, bf16[256,512]{1,0:T(8,128)(2,1)}), (bf16[256,512]{1,0:T(8,128)(2,1)}, bf16[256,512]{1,0:T(8,128)(2,1)})) %all-reduce.9.cloned.1.call-update) | async-done | bytes 524304 | tf_op jit(solution)/shard_map/psum | solution.py:15
  876.2 0.9 slice.63
  877.1 1.1 pad_maximum_fusion.4
  878.2 3.4 collective-permute-start.2
  881.6 1.3 collective-permute-start.3
  884.7 4.1 collective-permute-done.3
  890.2 92.4 %reduce-scatter.6.cloned.1.call-done = f32[16,512]{1,0:T(8,128)} async-done(((f32[256,512]{1,0:T(8,128)}), f32[16,512]{1,0:T(8,128)}) %reduce-scatter.6.cloned.1.call-update) | async-done | bytes 32784 | tf_op jit(solution)/shard_map/reduce_scatter | solution.py:107
  983.5 38.8 %all_gather.11 = bf16[256,512]{1,0:T(8,128)(2,1)S(1)} all-gather(bf16[16,512]{1,0:T(8,128)(2,1)S(1)} %get-tuple-element.56), channel_id=1, replica_groups=mesh['row'=32,'col'=16] {'col'}, dimensions={0}, use_global_device_ids=true | all-gather | bytes 278528 | tf_op jit(solution)/shard_map/all_gather | solution.py:93
  1023.2 336.3 %all-reduce.7.cloned.1.call-done = (bf16[256,512]{1,0:T(8,128)(2,1)}, bf16[256,512]{1,0:T(8,128)(2,1)}) async-done(((bf16[256,512]{1,0:T(8,128)(2,1)}, bf16[256,512]{1,0:T(8,128)(2,1)}), (bf16[256,512]{1,0:T(8,128)(2,1)}, bf16[256,512]{1,0:T(8,128)(2,1)})) %all-reduce.7.cloned.1.call-update) | async-done | bytes 524304 | tf_op jit(solution)/shard_map/psum | solution.py:15
  1361.4 1.1 pad_maximum_fusion.5
  1362.5 3.4 collective-permute-start.4
  1365.9 1.3 collective-permute-start.5
  1368.9 4.1 collective-permute-done.5
  1375.0 91.8 %reduce-scatter.8.cloned.1.call-done = f32[16,512]{1,0:T(8,128)} async-done(((f32[256,512]{1,0:T(8,128)}), f32[16,512]{1,0:T(8,128)}) %reduce-scatter.8.cloned.1.call-update) | async-done | bytes 32784 | tf_op jit(solution)/shard_map/reduce_scatter | solution.py:107
  1466.7 1.4 multiply_add_fusion
  (103 shorter events, 20.4 us)
Async XLA Ops:
  7.2 392.0 %copy-start = (bf16[2,4,32,256]{3,2,1,0:T(8,128)(2,1)S(1)}, bf16[2,4,32,256]{3,2,1,0:T(8,128)(2,1)}, u32[]{:S(2)}) copy-start(bf16[2,4,32,256]{3,2,1,0:T(8,128)(2,1)} %param.21) | copy-start | bytes 393220
  7.2 384.0 %all-reduce.11.cloned.1.call-start = ((), (), s32[]{:S(2)}) async-start(), calls=%async_computation.8 | async-start | bytes 1048576 | tf_op jit(solution)/shard_map/psum | solution.py:15
  9.5 44.9 %copy-start.13 = (s32[2,4]{1,0:T(2,128)S(1)}, s32[2,4]{1,0:T(2,128)}, u32[]{:S(2)}) copy-start(s32[2,4]{1,0:T(2,128)} %param.23) | copy-start | bytes 100
  54.3 444.2 %reduce-scatter.4.cloned.1.call-start = ((), (), s32[]{:S(2)}) async-start(), calls=%async_computation.3 | async-start | bytes 557056 | tf_op jit(solution)/shard_map/reduce_scatter | solution.py:107
  393.0 6.2 copy-start.7
  394.1 6.4 collective-permute-start
  397.5 7.2 collective-permute-start.1
  399.7 5.0 copy-start.1
  399.7 5.0 copy-start.2
  399.9 4.8 copy-start.14
  404.8 1.2 copy-start.10
  405.8 92.8 %copy-start.9 = (s32[16,512]{1,0:T(8,128)S(1)}, s32[16,512]{1,0:T(8,128)}, u32[]{:S(2)}) copy-start(s32[16,512]{1,0:T(8,128)} %param.17) | copy-start | bytes 98308
  405.8 469.5 %all-reduce.9.cloned.1.call-start = ((), (), s32[]{:S(2)}) async-start(), calls=%async_computation.7 | async-start | bytes 1048576 | tf_op jit(solution)/shard_map/psum | solution.py:15
  539.1 443.6 %reduce-scatter.6.cloned.1.call-start = ((), (), s32[]{:S(2)}) async-start(), calls=%async_computation.4 | async-start | bytes 557056 | tf_op jit(solution)/shard_map/reduce_scatter | solution.py:107
  878.2 6.4 collective-permute-start.2
  881.6 7.2 collective-permute-start.3
  883.8 5.0 copy-start.5
  883.8 5.0 copy-start.6
  889.8 469.7 %all-reduce.7.cloned.1.call-start = ((), (), s32[]{:S(2)}) async-start(), calls=%async_computation.6 | async-start | bytes 1048576 | tf_op jit(solution)/shard_map/psum | solution.py:15
  1023.2 443.6 %reduce-scatter.8.cloned.1.call-start = ((), (), s32[]{:S(2)}) async-start(), calls=%async_computation.5 | async-start | bytes 557056 | tf_op jit(solution)/shard_map/reduce_scatter | solution.py:107
  1362.5 6.4 collective-permute-start.4
  1365.9 7.2 collective-permute-start.5
  1368.0 5.0 copy-start.3
  1368.0 5.0 copy-start.4
  (3 other events, 3.3 us)
Sparse Core Ops, SparseCore 0:
  54.4 336.6 all-reduce.10
  405.9 92.5 reduce-scatter.3
  539.2 336.0 all-reduce.8
  890.0 92.6 reduce-scatter.5
  1023.3 336.2 all-reduce.6
  1374.2 92.4 reduce-scatter.7
where the time goes:
time: 1480 us; the launch traced here: 1470 us
  waiting for transfers between devices  1300 us (88%)
  blocking collectives  122 us (8%)
    psum x3, waiting for transfers between devices, broadcast(): return lax.psum(kept, axis)  1010 us
    reduce_scatter x3, waiting for transfers between devices, tendency(): lax.psum_scatter(partial_value, 'col', scatter_dimension=0, tiled=True)  277 us
    all_gather x3, blocking collectives, tendency(): all_members = lax.all_gather(excess, 'col', axis=0, tiled=True)  122 us
  transfers between devices with their start and end apart: 12, of which 12 were waited for; matrix products, arithmetic and copies ran while one was open for 0% of the time, Pallas kernels for 0%

commit v1 on v0

v1 whole, which is shorter than its diff:
```python
import jax
import jax.numpy as jnp
from jax import lax
from jax.sharding import PartitionSpec as P

B = 128
HSTEP = 0.2
RATE_UNIT = 1.0 / 1024.0


def local(stress, state, load_rate, a_param, b_param, near_band, u_far, v_far, ranks):
    rows = lax.axis_size("row")
    row_index = lax.axis_index("row")
    col_index = lax.axis_index("col")
    block_rows, block_cols, slots, dofs = u_far.shape
    members = stress.shape[0]
    blocks = rows * block_rows

    global_rows = row_index * block_rows + jnp.arange(block_rows, dtype=jnp.int32)
    global_cols = col_index * block_cols + jnp.arange(block_cols, dtype=jnp.int32)
    distant = jnp.abs(global_rows[:, None] - global_cols[None, :]) >= 2
    active = (jnp.arange(slots, dtype=jnp.int32)[None, None, :] < ranks[:, :, None]) & distant[:, :, None]
    v_own = jnp.where(active[..., None], v_far, 0).astype(v_far.dtype)
    v_all = lax.all_gather(jnp.swapaxes(v_own, 0, 1), "col", axis=0, tiled=True)
    u_all = lax.all_gather(jnp.swapaxes(u_far, 0, 1), "col", axis=0, tiled=True)

    def to_blocks(value):
        return jnp.swapaxes(value.reshape(members, block_rows, -1), 0, 1)

    def from_blocks(value):
        return jnp.swapaxes(value, 0, 1).reshape(members, -1)

    plate = to_blocks(load_rate.astype(jnp.float32) * RATE_UNIT)
    stress_start, state_start = to_blocks(stress), to_blocks(state)
    direct = a_param.reshape(block_rows, 1, B)
    evolve = b_param.reshape(block_rows, 1, B)
    band = near_band.reshape(block_rows, dofs, 3, dofs)

    def tendency(stress_now, state_now):
        decay = jnp.exp(-state_now)
        rate_a = 2.0 * decay * jnp.sinh(stress_now[..., :B] / direct)
        rate_b = 2.0 * decay * jnp.sinh(stress_now[..., B:] / direct)
        drift = evolve * (decay - jnp.sqrt(rate_a * rate_a + rate_b * rate_b))
        excess = (jnp.concatenate([rate_a, rate_b], axis=2) - plate).astype(jnp.bfloat16)
        copies = jnp.broadcast_to(excess[None], (rows,) + excess.shape)
        grid = lax.all_to_all(copies, "row", 0, 0).reshape(blocks, members, dofs)
        weights = jnp.einsum("jmd,jird->jmir", grid, v_all, preferred_element_type=jnp.float32)
        weights = weights.astype(jnp.bfloat16)
        total = jnp.einsum("jmir,jird->imd", weights, u_all, preferred_element_type=jnp.float32)
        window = []
        for offset in range(-1, block_rows + 1):
            at = row_index * block_rows + offset
            block = lax.dynamic_index_in_dim(grid, jnp.clip(at, 0, blocks - 1), 0, keepdims=False)
            window.append(jnp.where((at >= 0) & (at < blocks), block, 0).astype(block.dtype))
        windows = jnp.stack([jnp.stack(window[i : i + 3]) for i in range(block_rows)])
        total = total + jnp.einsum("ismd,iksd->imk", windows, band, preferred_element_type=jnp.float32)
        return -total, drift

    rate_one, drift_one = tendency(stress_start, state_start)
    stress_one = stress_start + HSTEP * rate_one
    state_one = state_start + HSTEP * drift_one
    rate_two, drift_two = tendency(stress_one, state_one)
    stress_two = 0.75 * stress_start + 0.25 * (stress_one + HSTEP * rate_two)
    state_two = 0.75 * state_start + 0.25 * (state_one + HSTEP * drift_two)
    rate_three, drift_three = tendency(stress_two, state_two)
    new_stress = stress_start / 3.0 + 2.0 / 3.0 * (stress_two + HSTEP * rate_three)
    new_state = state_start / 3.0 + 2.0 / 3.0 * (state_two + HSTEP * drift_three)
    return from_blocks(new_stress), from_blocks(new_state)


def solution(mesh):
    return jax.shard_map(
        local,
        mesh=mesh,
        in_specs=(
            P("col", "row"),
            P("col", "row"),
            P("col", "row"),
            P("row"),
            P("row"),
            P("row", None),
            P("row", "col", None, None),
            P("row", "col", None, None),
            P("row", "col"),
        ),
        out_specs=(P("col", "row"), P("col", "row")),
        check_vma=False,
    )
```

time: 1480 us -> 267 us (0.18)
  the two profiles are of different devices: /device:TPU:64 before, /device:TPU:8 now
where the time goes in v1:
time: 267 us; the launch traced here: 266 us
  waiting for transfers between devices  173 us (65%)
  blocking collectives  34.7 us (13%)
  starting transfers between devices  19.2 us (7%)
  matrix products  14.2 us (5%)
  between operations  14.2 us (5%)
  local copies, waits for them, and re-layouts  6.56 us (2%)
  other arithmetic  3.55 us (1%)
    all_gather x1, waiting for transfers between devices, local(): u_all = lax.all_gather(jnp.swapaxes(u_far, 0, 1), 'col', axis=0, tiled=True)  85 us
    all_to_all x2, waiting for transfers between devices, tendency(): grid = lax.all_to_all(copies, 'row', 0, 0).reshape(blocks, members, dofs)  47.9 us
    all_gather x1, waiting for transfers between devices, local(): v_all = lax.all_gather(jnp.swapaxes(v_own, 0, 1), 'col', axis=0, tiled=True)  40.5 us
    all_to_all x1, blocking collectives, tendency(): grid = lax.all_to_all(copies, 'row', 0, 0).reshape(blocks, members, dofs)  34.7 us
    all_to_all x2, starting transfers between devices, tendency(): grid = lax.all_to_all(copies, 'row', 0, 0).reshape(blocks, members, dofs)  19.1 us
    dot_general x3, matrix products, tendency(): jnp.einsum('jmir,jird->imd', weights, u_all, preferred_element_type=jnp.f...  10.8 us
  transfers between devices with their start and end apart: 4, of which 4 were waited for; matrix products, arithmetic and copies ran while one was open for 2% of the time, Pallas kernels for 0%

profile of v1, /device:TPU:8, one launch (start us, length us, event | category | flops | bytes accessed | tf_op | source)
XLA Modules:
  0.0 266.0 jit_solution(15811500693297151694)
XLA Ops:
  7.3 0.8 copy.54
  8.2 1.7 fusion.23
  10.0 1.6 copy.106
  11.6 0.8 copy.107
  12.3 0.8 convert_multiply_fusion
  13.1 0.8 fusion.62
  13.9 0.9 broadcast_in_dim.51
  14.7 15.2 %all-to-all-start = ((bf16[32,2,16,256]{3,2,1,0:T(8,128)(2,1)}), bf16[32,2,16,256]{3,2,1,0:T(8,128)(2,1)S(1)}, u32[]{:S(2)}, u32[]{:S(2)}) async-start(bf16[32,2,16,256]{3,2,1,0:T(8,128)(2,1)} %broadcast_in_dim.51), calls=%async_computation | async-start | bytes 1048576 | tf_op jit(solution)/shard_map/all_to_all | solution.py:46
  30.0 0.4 reshape.98
  30.4 25.7 %all-to-all-done = bf16[32,2,16,256]{3,2,1,0:T(8,128)(2,1)S(1)} async-done(((bf16[32,2,16,256]{3,2,1,0:T(8,128)(2,1)}), bf16[32,2,16,256]{3,2,1,0:T(8,128)(2,1)S(1)}, u32[]{:S(2)}, u32[]{:S(2)}) %all-to-all-start) | async-done | bytes 524320 | tf_op jit(solution)/shard_map/all_to_all | solution.py:46
  56.1 0.3 convolution_bitcast_fusion.2
  56.4 40.5 %all-gather.3.cloned.1.call-done = bf16[64,2,32,256]{3,2,1,0:T(8,128)(2,1)} async-done(((bf16[4,2,32,256]{3,2,1,0:T(8,128)(2,1)}), bf16[64,2,32,256]{3,2,1,0:T(8,128)(2,1)}) %all-gather.3.cloned.1.call-update) | async-done | bytes 2097168 | tf_op jit(solution)/shard_map/all_gather | solution.py:24
  97.0 85.0 %all-gather.5.cloned.1.call-done = bf16[64,2,32,256]{3,2,1,0:T(8,128)(2,1)} async-done(((bf16[4,2,32,256]{3,2,1,0:T(8,128)(2,1)}), bf16[64,2,32,256]{3,2,1,0:T(8,128)(2,1)}) %all-gather.5.cloned.1.call-update) | async-done | bytes 2097168 | tf_op jit(solution)/shard_map/all_gather | solution.py:25
  182.1 4.0 %fusion.73 = (f32[2,16,256]{2,1,0:T(8,128)S(1)}, f32[2,16,256]{2,1,0:T(8,128)S(1)}) fusion(f32[2,2,8,256]{3,2,1,0:T(8,128)S(1)} %bitcast.238, f32[2,16,256]{2,1,0:T(8,128)S(1)} %convolution_bitcast_fusion.2, bf16[64,2,32,256]{3,2,1,0:T(8,128)(2,1)} %all-gather.5.cloned.1.call-done, bf16[64,16,256,1]{2,1,3,0:T(8,128)(2,1)S(1)} %bitcast.232, ...), kind=kOutput, calls=%fused_computation.132 | convolution fusion | flops 67207168 | bytes 4849664 | tf_op jit(solution)/shard_map/jmir,jird->imd/dot_general | solution.py:49
  186.3 34.7 %all_to_all.15 = bf16[32,2,16,256]{3,2,1,0:T(8,128)(2,1)S(1)} all-to-all(bf16[32,2,16,256]{3,2,1,0:T(8,128)(2,1)S(1)} %broadcast_in_dim.55), channel_id=1, replica_groups=mesh['row'=32,'col'=16] {'row'}, dimensions={0} | all-to-all | bytes 1048576 | tf_op jit(solution)/shard_map/all_to_all | solution.py:46
  221.0 1.5 convolution_bitcast_fusion.1
  222.6 3.4 %multiply_add_fusion = (f32[2,16,256]{2,1,0:T(8,128)S(1)}, f32[2,16,256]{2,1,0:T(8,128)S(1)}) fusion(f32[2,2,8,256]{3,2,1,0:T(8,128)S(1)} %bitcast.239, f32[2,16,256]{2,1,0:T(8,128)S(1)} %get-tuple-element.30, f32[2,16,256]{2,1,0:T(8,128)S(1)} %convolution_bitcast_fusion.1, bf16[64,2,32,256]{3,2,1,0:T(8,128)(2,1)} %all-gather.5.cloned.1.call-done, ...), kind=kOutput, calls=%fused_computation.55 | convolution fusion | flops 67239936 | bytes 4882432 | tf_op jit(solution)/shard_map/jmir,jird->imd/dot_general | solution.py:49
  226.1 0.9 broadcast_in_dim.56
  226.9 3.9 %all-to-all-start.2 = ((bf16[32,2,16,256]{3,2,1,0:T(8,128)(2,1)}), bf16[32,2,16,256]{3,2,1,0:T(8,128)(2,1)S(1)}, u32[]{:S(2)}, u32[]{:S(2)}) async-start(bf16[32,2,16,256]{3,2,1,0:T(8,128)(2,1)} %broadcast_in_dim.56), calls=%async_computation.2 | async-start | bytes 1048576 | tf_op jit(solution)/shard_map/all_to_all | solution.py:46
  230.8 0.6 copy.108
  231.4 22.1 %all-to-all-done.2 = bf16[32,2,16,256]{3,2,1,0:T(8,128)(2,1)S(1)} async-done(((bf16[32,2,16,256]{3,2,1,0:T(8,128)(2,1)}), bf16[32,2,16,256]{3,2,1,0:T(8,128)(2,1)S(1)}, u32[]{:S(2)}, u32[]{:S(2)}) %all-to-all-start.2) | async-done | bytes 524320 | tf_op jit(solution)/shard_map/all_to_all | solution.py:46
  253.6 1.5 convolution_bitcast_fusion
  255.1 3.4 %fusion.11 = f32[2,2,8,256]{3,2,1,0:T(8,128)S(1)} fusion(f32[2,16,256]{2,1,0:T(8,128)S(1)} %convolution_bitcast_fusion, bf16[64,2,32,256]{3,2,1,0:T(8,128)(2,1)} %all-gather.5.cloned.1.call-done, bf16[64,16,256,1]{2,1,3,0:T(8,128)(2,1)S(1)} %bitcast.234, bf16[64,2,32,256]{3,2,1,0:T(8,128)(2,1)S(1)} %copy-done.1, f32[2,16,256]{2,1,0:T(8,128)S(1)} %get-tuple-element.32, ...), kind=kOutput, calls=%fused_computation.14 | convolution fusion | flops 67272704 | bytes 4882432 | tf_op jit(solution)/shard_map/jmir,jird->imd/dot_general | solution.py:49
  258.5 0.6 copy.75
  (34 shorter events, 0.6 us)
Async XLA Ops:
  7.2 5.9 %copy-start = (f32[16,256]{1,0:T(8,128)S(1)}, f32[16,256]{1,0:T(8,128)}, u32[]{:S(2)}) copy-start(f32[16,256]{1,0:T(8,128)} %param.10) | copy-start | bytes 49156
  7.2 22.8 %copy-start.3 = (bf16[512,768]{1,0:T(8,128)(2,1)S(1)}, bf16[512,768]{1,0:T(8,128)(2,1)}, u32[]{:S(2)}) copy-start(bf16[512,768]{1,0:T(8,128)(2,1)} %param.14) | copy-start | bytes 2359300
  7.2 89.8 %all-gather.3.cloned.1.call-start = ((), (), s32[]{:S(2)}) async-start(), calls=%async_computation.3 | async-start | bytes 2228224 | tf_op jit(solution)/shard_map/all_gather | solution.py:24
  9.9 172.1 %all-gather.5.cloned.1.call-start = ((), (), s32[]{:S(2)}) async-start(), calls=%async_computation.4 | async-start | bytes 2228224 | tf_op jit(solution)/shard_map/all_gather | solution.py:25
  14.7 167.3 %copy-start.4 = (f32[16,512]{1,0:T(8,128)S(1)}, f32[16,512]{1,0:T(8,128)}, u32[]{:S(2)}) copy-start(f32[16,512]{1,0:T(8,128)} %param.9) | copy-start | bytes 98308
  14.7 41.4 %all-to-all-start = ((bf16[32,2,16,256]{3,2,1,0:T(8,128)(2,1)}), bf16[32,2,16,256]{3,2,1,0:T(8,128)(2,1)S(1)}, u32[]{:S(2)}, u32[]{:S(2)}) async-start(bf16[32,2,16,256]{3,2,1,0:T(8,128)(2,1)} %broadcast_in_dim.51), calls=%async_computation | async-start | bytes 1048576 | tf_op jit(solution)/shard_map/all_to_all | solution.py:46
  30.3 151.7 %copy-start.2 = (bf16[2,256,3,256]{3,2,1,0:T(4,128)(2,1)}, bf16[2,256,3,256]{3,2,1,0:T(4,128)(2,1)S(1)}, u32[]{:S(2)}) copy-start(bf16[2,256,3,256]{3,2,1,0:T(4,128)(2,1)S(1)} %reshape.98) | copy-start | bytes 2359300
  182.0 4.1 %copy-start.5 = (f32[256]{0:T(256)S(1)}, f32[256]{0:T(256)}, u32[]{:S(2)}) copy-start(f32[256]{0:T(256)} %param.13) | copy-start | bytes 3076
  182.1 4.1 %copy-start.6 = (f32[256]{0:T(256)S(1)}, f32[256]{0:T(256)}, u32[]{:S(2)}) copy-start(f32[256]{0:T(256)} %param.12) | copy-start | bytes 3076
  186.1 36.5 %copy-start.1 = (bf16[64,2,32,256]{3,2,1,0:T(8,128)(2,1)S(1)}, bf16[64,2,32,256]{3,2,1,0:T(8,128)(2,1)}, u32[]{:S(2)}) copy-start(bf16[64,2,32,256]{3,2,1,0:T(8,128)(2,1)} %all-gather.3.cloned.1.call-done) | copy-start | bytes 6291460
  226.9 26.6 %all-to-all-start.2 = ((bf16[32,2,16,256]{3,2,1,0:T(8,128)(2,1)}), bf16[32,2,16,256]{3,2,1,0:T(8,128)(2,1)S(1)}, u32[]{:S(2)}, u32[]{:S(2)}) async-start(bf16[32,2,16,256]{3,2,1,0:T(8,128)(2,1)} %broadcast_in_dim.56), calls=%async_computation.2 | async-start | bytes 1048576 | tf_op jit(solution)/shard_map/all_to_all | solution.py:46
Sparse Core Ops, SparseCore 0:
  10.1 86.8 all-gather.2
  99.1 82.9 all-gather.4
